TPU v7x, 32 devices: a whole 2x2x4 slice. The times are simulated.
32 devices in a mesh: groups: 2 (over y), width: 4 (over z), store: 4 (over x, core).
Axes of the slice: x: 2, y: 2, z: 4, core: 2. Of those that a mesh axis runs over, the one named last changes fastest.
Arguments:
- activations: bfloat16 [8192, 8192], P(('groups', 'store'), 'width'), parts along dimension 0, may hold values from -6 to 6
- out_grads: bfloat16 [8192, 8192], P(('groups', 'store'), 'width'), parts along dimension 0, may hold values from -6 to 6
- example_of: int32 [8, 1024], P(('groups', 'store')), parts along dimension 0, may hold values from 0 to 127, never falling along the last dimension, each value on 1 to 16 neighbouring positions
- proj_in: bfloat16 [8192, 64], P('width'), may hold values from -0.0625 to 0.0625
- proj_out: bfloat16 [8192, 64], P('width'), may hold values from -0.0625 to 0.0625
- inverse_curvature: bfloat16 [4096, 4096], P('width'), may hold values from -1 to 3
- stored: bfloat16 [4096, 4096], P(('width', 'store')), may hold values from -0.3984375 to 0.3984375
Outputs:
- scores: float32 [1024, 4096], P('groups', ('width', 'store')), parts along dimension 0
There are 2 independent parts, one for each index of `groups`. A program takes and returns all parts, laid end to end along the dimension named above; an argument that names none is the same for every part. Nothing has to cross between parts.
Inputs may be any that keep to these rules, and one draw needn't show every extreme that they name: `example_of`: the tokens of one example are consecutive; every example of 0 to 127 has 1 to 16 tokens in each row.
All inputs are finite; a program needn't handle non-finite values.
Results may differ from a plain program's by a relative error of at most 0.0057.
Values may be sent and summed in bfloat16 or wider, within the bound.
A program may use at most 64 MiB of HBM per device.

v0:
```python
import functools

import jax
import jax.numpy as jnp
from jax import lax
from jax.experimental import pallas as pl
from jax.experimental.pallas import tpu as pltpu
from jax.sharding import PartitionSpec as P

EX_DEV = 128
F32 = jnp.float32
BF16 = jnp.bfloat16
NT = (((1,), (1,)), ((), ()))


def kernel(cfg, act_hbm, grad_hbm, ids_ref, pin_hbm, pout_hbm, inv_hbm, st_hbm, out_ref,
           act, grad, w_in, w_out, inv, st, sbuf, rbuf, fac, expand, pex, query,
           local_sem, rs_send, rs_recv, ag_send, ag_recv, z_send, h_send, q_recv):
    width, store, chunk, pieces, piece = cfg
    rank = pin_hbm.shape[0]
    ex = EX_DEV
    me = lax.axis_index("width")
    my_store = lax.axis_index("store")
    bits = [1 << b for b in reversed(range(store.bit_length() - 1))]

    def wrap(x):
        return lax.rem(x, width)

    def rows(c):
        return pl.ds(pl.multiple_of(c * chunk, chunk), chunk)

    def remote(src, dst, send, recv, **where):
        return pltpu.make_async_remote_copy(
            src_ref=src, dst_ref=dst, send_sem=send, recv_sem=recv,
            device_id=where, device_id_type=pl.DeviceIdType.MESH)

    loads_w = [
        pltpu.make_async_copy(pin_hbm, w_in.at[pl.ds(0, rank)], local_sem.at[0]),
        pltpu.make_async_copy(pout_hbm, w_out.at[pl.ds(rank, rank)], local_sem.at[1]),
    ]
    for copy in loads_w:
        copy.start()
    loads = []
    for k in range(width):
        c = wrap(me + 1 + k)
        pair = (
            pltpu.make_async_copy(act_hbm.at[rows(c)], act.at[k], local_sem.at[4 + 2 * k]),
            pltpu.make_async_copy(grad_hbm.at[rows(c)], grad.at[k], local_sem.at[5 + 2 * k]),
        )
        for copy in pair:
            copy.start()
        loads.append(pair)
    load_inv = pltpu.make_async_copy(inv_hbm, inv, local_sem.at[2])
    load_st = pltpu.make_async_copy(st_hbm, st, local_sem.at[3])

    barrier = pltpu.get_barrier_semaphore()
    for k in range(1, width):
        pl.semaphore_signal(barrier, inc=1, device_id={"width": wrap(me + k)},
                            device_id_type=pl.DeviceIdType.MESH)
    for bit in bits:
        pl.semaphore_signal(barrier, inc=1, device_id={"store": partner(my_store, bit)},
                            device_id_type=pl.DeviceIdType.MESH)

    w_in[rank:, :] = jnp.zeros((rank, w_in.shape[1]), BF16)
    w_out[:rank, :] = jnp.zeros((rank, w_out.shape[1]), BF16)
    feat = expand.shape[1]
    row_at = lax.broadcasted_iota(jnp.int32, (2 * rank, feat), 0)
    col_at = lax.broadcasted_iota(jnp.int32, (2 * rank, feat), 1)
    expand[...] = jnp.where(row_at - rank == col_at // rank, 1.0, 0.0).astype(BF16)

    pl.semaphore_wait(barrier, width - 1 + len(bits))
    for copy in loads_w:
        copy.wait()

    own = None
    rs_copies = []
    for k in range(width):
        for copy in loads[k]:
            copy.wait()
        part = (lax.dot_general(act[k], w_in[...], NT, preferred_element_type=F32)
                + lax.dot_general(grad[k], w_out[...], NT, preferred_element_type=F32))
        if k < width - 1:
            sbuf[k] = part.astype(BF16)
            copy = remote(sbuf.at[k], rbuf.at[k], rs_send.at[k], rs_recv.at[k],
                          width=wrap(me + 1 + k))
            copy.start()
            rs_copies.append(copy)
        else:
            own = part
    load_inv.start()
    load_st.start()
    for k in range(width - 1):
        rs_copies[k].wait_recv()
        own = own + rbuf[k].astype(F32)
    fac[rows(me), :] = own.astype(BF16)
    ag_copies = []
    for k in sorted(range(width - 1), key=lambda k: abs(2 * (k + 1) - width)):
        copy = remote(fac.at[rows(me)], fac.at[rows(me)], ag_send.at[k], ag_recv.at[k],
                      width=wrap(me + 1 + k))
        copy.start()
        ag_copies.append(copy)
    member = ids_ref[...] == lax.broadcasted_iota(jnp.int32, (ex, ids_ref.shape[1]), 0)
    counts = jnp.sum(member.astype(F32), axis=1, keepdims=True)
    member = member.astype(F32).astype(BF16)
    for k in range(width - 1):
        sender = wrap(me + width - 1 - k)
        remote(fac.at[rows(me)], fac.at[rows(sender)], ag_send.at[k], ag_recv.at[k],
               width=sender).wait_recv()

    tile_row = lax.broadcasted_iota(jnp.int32, (2 * rank, 2 * rank), 0)
    tile_col = lax.broadcasted_iota(jnp.int32, (2 * rank, 2 * rank), 1)
    twice = jnp.where(tile_row == lax.rem(tile_col, rank), 1.0, 0.0).astype(BF16)
    block = 512
    act_twice = jnp.dot(fac[...], twice, preferred_element_type=F32)
    act_block = jnp.concatenate([act_twice] * (block // (2 * rank)), axis=1)

    @pl.loop(0, feat // block, unroll=True)
    def _(n):
        cols = pl.ds(pl.multiple_of(n * block, block), block)
        spread = jnp.dot(fac[...], expand[:, cols], preferred_element_type=F32)
        token_outer = (spread * act_block).astype(BF16)
        total = jnp.dot(member, token_outer, preferred_element_type=F32)
        pex[:, cols] = (total / counts).astype(BF16)

    load_inv.wait()
    load_st.wait()

    def seat(s):
        return pl.ds(pl.multiple_of(s * ex, ex), ex)

    def held(w, p, s):
        return query.at[w * pieces + p, seat(s)]

    def along_width(w, p, to, sem):
        return remote(held(w, p, my_store), held(w, p, my_store), z_send.at[sem],
                      q_recv.at[w * pieces + p, my_store], width=to)

    def along_store(w, p, stage, index, s):
        bit = bits[stage]
        to = partner(my_store, bit)
        return remote(held(w, p, s), held(w, p, s),
                      h_send.at[w * pieces + p, (1 << stage) - 1 + index],
                      q_recv.at[w * pieces + p, s], store=to)

    def groups(stage):
        out = [my_store]
        for bit in bits[:stage]:
            out = out + [partner(s, bit) for s in out]
        return out

    def arrived(w, p, s):
        remote(held(w, p, s), held(w, p, s), z_send.at[0], q_recv.at[w * pieces + p, s],
               width=me).wait_recv()

    n_bits = len(bits)

    def spread_own(w, p):
        for stage in range(n_bits):
            along_store(w, p, stage, 0, my_store).start()

    def spread_from(w, p, stage):
        bit = bits[stage]
        for index, s in enumerate(groups(stage)):
            source = partner(s, bit)
            arrived(w, p, source)
            for later in range(stage + 1, n_bits):
                along_store(w, p, later, (1 << stage) + index, source).start()

    for p in range(pieces):
        value = lax.dot_general(pex[...], inv[p * piece:(p + 1) * piece, :], NT,
                                preferred_element_type=F32)
        query[me * pieces + p, seat(my_store), :] = value.astype(BF16)

        @pl.when(me + 1 < width)
        def _():
            along_width(me, p, me + 1, me * pieces + p).start()

        @pl.when(me > 0)
        def _():
            along_width(me, p, me - 1, width * pieces + p).start()

        spread_own(me, p)

    def scores_of(w, p, first):
        cols = pl.ds(pl.multiple_of((w * pieces + p) * piece, piece), piece)
        value = lax.dot_general(query[w * pieces + p], st[:, cols], NT, preferred_element_type=F32)
        if first:
            out_ref[...] = value
        else:
            out_ref[...] += value

    def sides(d):
        if d == 0:
            return [(me, None)]
        return [(me - d, me - d >= 0), (me + d, me + d < width)]

    def guarded(ok, fn):
        if ok is None:
            fn()
        else:
            pl.when(ok)(fn)

    for step in range(width + n_bits):
        for p in range(pieces):
            if 1 <= step < width:
                for side, (w, ok) in enumerate(sides(step)):
                    def take(w=w, side=side, p=p):
                        arrived(w, p, my_store)
                        if side == 0:
                            @pl.when(me + 1 < width)
                            def _():
                                along_width(w, p, me + 1, w * pieces + p).start()
                        else:
                            @pl.when(me > 0)
                            def _():
                                along_width(w, p, me - 1, w * pieces + p).start()
                        spread_own(w, p)
                    guarded(ok, take)
            for stage in range(n_bits):
                d = step - 1 - stage
                if 0 <= d < width:
                    for w, ok in sides(d):
                        guarded(ok, functools.partial(spread_from, w, p, stage))
            d = step - n_bits
            if 0 <= d < width:
                for w, ok in sides(d):
                    guarded(ok, functools.partial(scores_of, w, p, d == 0 and p == 0))

    for copy in rs_copies:
        copy.wait_send()
    for copy in ag_copies:
        copy.wait_send()
    for p in range(pieces):
        @pl.when(me + 1 < width)
        def _():
            along_width(me, p, me + 1, me * pieces + p).wait_send()

        @pl.when(me > 0)
        def _():
            along_width(me, p, me - 1, width * pieces + p).wait_send()

        for w in range(width):
            @pl.when(jnp.logical_and(w < me, me + 1 < width))
            def _():
                along_width(w, p, me + 1, w * pieces + p).wait_send()

            @pl.when(jnp.logical_and(w > me, me > 0))
            def _():
                along_width(w, p, me - 1, w * pieces + p).wait_send()

            for stage in range(n_bits):
                for index in range(1 << stage):
                    along_store(w, p, stage, index, my_store).wait_send()


def partner(s, bit):
    return s + bit - 2 * bit * lax.rem(s // bit, 2)


def body(activations, out_grads, example_of, proj_in, proj_out, inverse_curvature, stored):
    width = lax.axis_size("width")
    store = lax.axis_size("store")
    tokens, depth = activations.shape
    rank = proj_in.shape[1]
    part, feat = inverse_curvature.shape
    chunk = tokens // width
    piece = min(part, 256)
    pieces = part // piece
    n_rows = stored.shape[0]
    assert store & (store - 1) == 0
    hbm = pl.BlockSpec(memory_space=pl.ANY)
    vmem = pl.BlockSpec(memory_space=pltpu.VMEM)
    dma = pltpu.SemaphoreType.DMA
    return pl.pallas_call(
        functools.partial(kernel, (width, store, chunk, pieces, piece)),
        out_shape=jax.ShapeDtypeStruct((store * EX_DEV, n_rows), F32),
        in_specs=[hbm, hbm, vmem, hbm, hbm, hbm, hbm],
        out_specs=vmem,
        scratch_shapes=[
            pltpu.VMEM((width, chunk, depth), BF16),
            pltpu.VMEM((width, chunk, depth), BF16),
            pltpu.VMEM((2 * rank, depth), BF16),
            pltpu.VMEM((2 * rank, depth), BF16),
            pltpu.VMEM((part, feat), BF16),
            pltpu.VMEM((n_rows, feat), BF16),
            pltpu.VMEM((width - 1, chunk, 2 * rank), BF16),
            pltpu.VMEM((width - 1, chunk, 2 * rank), BF16),
            pltpu.VMEM((tokens, 2 * rank), BF16),
            pltpu.VMEM((2 * rank, feat), BF16),
            pltpu.VMEM((EX_DEV, feat), BF16),
            pltpu.VMEM((width * pieces, store * EX_DEV, piece), BF16),
            dma((4 + 2 * width,)),
            dma((width - 1,)),
            dma((width - 1,)),
            dma((width - 1,)),
            dma((width - 1,)),
            dma(((width + 1) * pieces,)),
            dma((width * pieces, store - 1)),
            dma((width * pieces, store)),
        ],
        compiler_params=pltpu.CompilerParams(
            collective_id=0, has_side_effects=True, vmem_limit_bytes=60 * 1024 * 1024),
        name="logra",
    )(activations, out_grads, example_of, proj_in.T, proj_out.T, inverse_curvature, stored)


def solution(mesh):
    return jax.shard_map(
        body,
        mesh=mesh,
        in_specs=(
            P(("groups", "store"), "width"),
            P(("groups", "store"), "width"),
            P(("groups", "store"), None),
            P("width", None),
            P("width", None),
            P("width", None),
            P(("width", "store"), None),
        ),
        out_specs=P("groups", ("width", "store")),
        check_vma=False,
    )
```

profile of v0, /device:TPU:0, one launch (start us, length us, event | category | flops | bytes accessed | tf_op | source)
XLA Modules:
  0.0 54.4 jit_solution(6604793062833601136)
XLA Ops:
  0.0 52.5 %logra.1 = f32[512,256]{1,0:T(8,128)} custom-call(bf16[1024,2048]{1,0:T(8,128)(2,1)} %act_hbm.1, bf16[1024,2048]{1,0:T(8,128)(2,1)} %grad_hbm.1, s32[1,1024]{1,0:T(1,128)} %ids_ref.1, bf16[64,2048]{1,0:T(8,128)(2,1)} %bitcast.2, bf16[64,2048]{1,0:T(8,128)(2,1)} %bitcast.3, bf16[1024,4096]{1,0:T(8,128)(2,1)} %inv_hbm.1, bf16[256,4096]{1,0:T(8,128)(2,1)} %st_hbm.1), custom_call_target="tpu_custom_call" | custom-call | tf_op jit(solution)/shard_map/logra/pallas_call | solution.py:274
  52.5 1.9 %copy.9 = f32[512,256]{1,0:T(8,128)} copy(f32[512,256]{1,0:T(8,128)} %logra.1) | data formatting | bytes 1048576
where the time goes:
time: 55.1 us; the launch traced here: 54.4 us
  Pallas kernels  52.5 us (95%)
  local copies, waits for them, and re-layouts  1.87 us (3%)
    pallas_call x1, Pallas kernels, body(): pl.pallas_call(functools.partial(kernel, (width, store, chunk, pieces, pi...  52.5 us
    unnamed x1, local copies, waits for them, and re-layouts  1.87 us

commit v1 on v0

--- a/solution.py
+++ b/solution.py
@@ -14,7 +14,7 @@
 
 
 def kernel(cfg, act_hbm, grad_hbm, ids_ref, pin_hbm, pout_hbm, inv_hbm, st_hbm, out_ref,
-           act, grad, w_in, w_out, inv, st, sbuf, rbuf, fac, expand, pex, query,
+           act, grad, w_in, w_out, inv, st, sbuf, rbuf, fac, expand, member, acc, pex, query,
            local_sem, rs_send, rs_recv, ag_send, ag_recv, z_send, h_send, q_recv):
     width, store, chunk, pieces, piece = cfg
     rank = pin_hbm.shape[0]
@@ -68,7 +68,13 @@
     col_at = lax.broadcasted_iota(jnp.int32, (2 * rank, feat), 1)
     expand[...] = jnp.where(row_at - rank == col_at // rank, 1.0, 0.0).astype(BF16)
 
-    pl.semaphore_wait(barrier, width - 1 + len(bits))
+    ids = ids_ref[...]
+    example = lax.broadcasted_iota(jnp.int32, (ex, chunk), 0)
+    counts = jnp.zeros((ex, 1), F32)
+    for c in range(width):
+        mine = (ids[:, c * chunk:(c + 1) * chunk] == example).astype(F32)
+        counts = counts + jnp.sum(mine, axis=1, keepdims=True)
+        member[c] = mine.astype(BF16)
     for copy in loads_w:
         copy.wait()
 
@@ -77,18 +83,22 @@
     for k in range(width):
         for copy in loads[k]:
             copy.wait()
+        if k == width - 1:
+            load_inv.start()
+            load_st.start()
         part = (lax.dot_general(act[k], w_in[...], NT, preferred_element_type=F32)
                 + lax.dot_general(grad[k], w_out[...], NT, preferred_element_type=F32))
         if k < width - 1:
             sbuf[k] = part.astype(BF16)
             copy = remote(sbuf.at[k], rbuf.at[k], rs_send.at[k], rs_recv.at[k],
                           width=wrap(me + 1 + k))
-            copy.start()
             rs_copies.append(copy)
         else:
             own = part
-    load_inv.start()
-    load_st.start()
+        if k == max(width - 2, 0):
+            pl.semaphore_wait(barrier, width - 1 + len(bits))
+            for copy in rs_copies:
+                copy.start()
     for k in range(width - 1):
         rs_copies[k].wait_recv()
         own = own + rbuf[k].astype(F32)
@@ -99,28 +109,49 @@
                       width=wrap(me + 1 + k))
         copy.start()
         ag_copies.append(copy)
-    member = ids_ref[...] == lax.broadcasted_iota(jnp.int32, (ex, ids_ref.shape[1]), 0)
-    counts = jnp.sum(member.astype(F32), axis=1, keepdims=True)
-    member = member.astype(F32).astype(BF16)
-    for k in range(width - 1):
-        sender = wrap(me + width - 1 - k)
-        remote(fac.at[rows(me)], fac.at[rows(sender)], ag_send.at[k], ag_recv.at[k],
-               width=sender).wait_recv()
 
     tile_row = lax.broadcasted_iota(jnp.int32, (2 * rank, 2 * rank), 0)
     tile_col = lax.broadcasted_iota(jnp.int32, (2 * rank, 2 * rank), 1)
     twice = jnp.where(tile_row == lax.rem(tile_col, rank), 1.0, 0.0).astype(BF16)
     block = 512
-    act_twice = jnp.dot(fac[...], twice, preferred_element_type=F32)
-    act_block = jnp.concatenate([act_twice] * (block // (2 * rank)), axis=1)
-
-    @pl.loop(0, feat // block, unroll=True)
-    def _(n):
-        cols = pl.ds(pl.multiple_of(n * block, block), block)
-        spread = jnp.dot(fac[...], expand[:, cols], preferred_element_type=F32)
-        token_outer = (spread * act_block).astype(BF16)
-        total = jnp.dot(member, token_outer, preferred_element_type=F32)
-        pex[:, cols] = (total / counts).astype(BF16)
+
+    def add_tokens(c, first, last):
+        factors = fac[rows(c), :]
+        act_twice = jnp.dot(factors, twice, preferred_element_type=F32)
+        act_block = jnp.concatenate([act_twice] * (block // (2 * rank)), axis=1)
+        for n in range(feat // block):
+            cols = slice(n * block, (n + 1) * block)
+            spread = jnp.dot(factors, expand[:, cols], preferred_element_type=F32)
+            token_outer = (spread * act_block).astype(BF16)
+            total = jnp.dot(member[c], token_outer, preferred_element_type=F32)
+            if not first:
+                total = total + acc[:, cols]
+            if last:
+                pex[:, cols] = (total / counts).astype(BF16)
+            else:
+                acc[:, cols] = total
+
+    near = jnp.minimum(me, width - 1 - me)
+
+    def nearest(j):
+        both = j <= 2 * near
+        far = jnp.where(me == near, 1, -1)
+        side = jnp.where(both, 2 * lax.rem(j + 1, 2) - 1, far)
+        return me + side * jnp.where(both, (j + 1) // 2, j - near)
+
+    def add_arrived(j, last):
+        c = nearest(j)
+        k = wrap(me - c - 1 + width)
+        remote(fac.at[rows(me)], fac.at[rows(c)], ag_send.at[k], ag_recv.at[k], width=c).wait_recv()
+        add_tokens(c, False, last)
+
+    add_tokens(me, True, width == 1)
+    if width > 2:
+        @pl.loop(1, width - 1, unroll=width <= 4)
+        def _(j):
+            add_arrived(j, False)
+    if width > 1:
+        add_arrived(width - 1, True)
 
     load_inv.wait()
     load_st.wait()
@@ -287,6 +318,8 @@
             pltpu.VMEM((width - 1, chunk, 2 * rank), BF16),
             pltpu.VMEM((tokens, 2 * rank), BF16),
             pltpu.VMEM((2 * rank, feat), BF16),
+            pltpu.VMEM((width, EX_DEV, chunk), BF16),
+            pltpu.VMEM((EX_DEV, feat), F32),
             pltpu.VMEM((EX_DEV, feat), BF16),
             pltpu.VMEM((width * pieces, store * EX_DEV, piece), BF16),
             dma((4 + 2 * width,)),

time: 55.1 us -> 57 us (1.034)
  Pallas kernels: 52.5 us -> 54.9 us
    pallas_call x1, Pallas kernels: 52.5 us -> 54.9 us  [body(): pl.pallas_call(functools.partial(kernel, (width, store, chunk, pieces, pi...]
where the time goes in v1:
time: 57 us; the launch traced here: 56.8 us
  Pallas kernels  54.9 us (96%)
  local copies, waits for them, and re-layouts  1.87 us (3%)
    pallas_call x1, Pallas kernels, body(): pl.pallas_call(functools.partial(kernel, (width, store, chunk, pieces, pi...  54.9 us
    unnamed x1, local copies, waits for them, and re-layouts  1.87 us

profile of v1, /device:TPU:0, one launch (start us, length us, event | category | flops | bytes accessed | tf_op | source)
XLA Modules:
  0.0 56.8 jit_solution(13071243498759861971)
XLA Ops:
  0.0 54.9 %logra.1 = f32[512,256]{1,0:T(8,128)} custom-call(bf16[1024,2048]{1,0:T(8,128)(2,1)} %act_hbm.1, bf16[1024,2048]{1,0:T(8,128)(2,1)} %grad_hbm.1, s32[1,1024]{1,0:T(1,128)} %ids_ref.1, bf16[64,2048]{1,0:T(8,128)(2,1)} %bitcast.2, bf16[64,2048]{1,0:T(8,128)(2,1)} %bitcast.3, bf16[1024,4096]{1,0:T(8,128)(2,1)} %inv_hbm.1, bf16[256,4096]{1,0:T(8,128)(2,1)} %st_hbm.1), custom_call_target="tpu_custom_call" | custom-call | tf_op jit(solution)/shard_map/logra/pallas_call | solution.py:305
  54.9 1.9 %copy.9 = f32[512,256]{1,0:T(8,128)} copy(f32[512,256]{1,0:T(8,128)} %logra.1) | data formatting | bytes 1048576

commit v2 on v0

v2 whole, which is shorter than its diff:
```python
import functools

import jax
import jax.numpy as jnp
from jax import lax
from jax.experimental import pallas as pl
from jax.experimental.pallas import tpu as pltpu
from jax.sharding import PartitionSpec as P

EX_DEV = 128
F32 = jnp.float32
BF16 = jnp.bfloat16
NT = (((1,), (1,)), ((), ()))


def kernel(cfg, act_hbm, grad_hbm, ids_ref, pin_hbm, pout_hbm, inv_hbm, st_hbm, out_hbm,
           act, grad, w_in, w_out, inv, st, sbuf, rbuf, fac, expand, member, counts_ref, pex, query, acc,
           local_sem, rs_send, rs_recv, ag_send, ag_recv, z_send, z_recv, st_send, st_recv,
           out_send, out_recv, out_sem):
    width, store, groups, chunk, pieces, piece = cfg
    rank = pin_hbm.shape[0]
    ex = EX_DEV
    me = lax.axis_index("width")
    group = lax.axis_index("groups")
    my_store = lax.axis_index("store")
    bits = [1 << b for b in reversed(range(store.bit_length() - 1))]

    def wrap(x):
        return lax.rem(x, width)

    def rows(c):
        return pl.ds(pl.multiple_of(c * chunk, chunk), chunk)

    def remote(src, dst, send, recv, **where):
        return pltpu.make_async_remote_copy(
            src_ref=src, dst_ref=dst, send_sem=send, recv_sem=recv,
            device_id=where, device_id_type=pl.DeviceIdType.MESH)

    loads_w = [
        pltpu.make_async_copy(pin_hbm, w_in.at[pl.ds(0, rank)], local_sem.at[0]),
        pltpu.make_async_copy(pout_hbm, w_out.at[pl.ds(rank, rank)], local_sem.at[1]),
    ]
    for copy in loads_w:
        copy.start()
    loads = []
    for k in range(width):
        c = wrap(me + 1 + k)
        pair = (
            pltpu.make_async_copy(act_hbm.at[rows(c)], act.at[k], local_sem.at[4 + 2 * k]),
            pltpu.make_async_copy(grad_hbm.at[rows(c)], grad.at[k], local_sem.at[5 + 2 * k]),
        )
        if k < 2:
            for copy in pair:
                copy.start()
        loads.append(pair)
    load_inv = pltpu.make_async_copy(inv_hbm, inv, local_sem.at[2])
    load_st = pltpu.make_async_copy(st_hbm, st.at[my_store], local_sem.at[3])

    barrier = pltpu.get_barrier_semaphore()
    for k in range(1, width):
        pl.semaphore_signal(barrier, inc=1, device_id={"width": wrap(me + k)},
                            device_id_type=pl.DeviceIdType.MESH)
    for k in range(1, store):
        pl.semaphore_signal(barrier, inc=1, device_id={"store": lax.rem(my_store + k, store)},
                            device_id_type=pl.DeviceIdType.MESH)
    if groups == 2:
        pl.semaphore_signal(barrier, inc=1, device_id={"groups": 1 - group},
                            device_id_type=pl.DeviceIdType.MESH)

    w_in[rank:, :] = jnp.zeros((rank, w_in.shape[1]), BF16)
    w_out[:rank, :] = jnp.zeros((rank, w_out.shape[1]), BF16)
    feat = expand.shape[1]

    far = jnp.where(2 * me < width, 1, -1)
    near = jnp.minimum(me, width - 1 - me)
    span = inv_hbm.shape[0]
    chunks = width if width <= 4 else 1
    middle = st_hbm.shape[0] // 4
    side_rows = (st_hbm.shape[0] - middle) // 2
    my_halves = [group] if groups == 2 else [0, 1]

    def nearest(j):
        if j == 0:
            return me
        both = j <= 2 * near
        side = jnp.where(both, far if j % 2 else -far, far)
        return me + side * jnp.where(both, (j + 1) // 2, j - near)

    order = [nearest(j) for j in range(width)]

    def columns(w):
        return pl.ds(pl.multiple_of(w * span, span), span)

    def block_of(j):
        return columns(order[j]) if chunks == width else pl.ds(0, feat)

    def half(h):
        if isinstance(h, int) and h == 2:
            return pl.ds(side_rows, middle)
        return pl.ds(pl.multiple_of(h * (side_rows + middle), 16), side_rows)

    stored_sends = []

    def hold(s, h, j):
        return st.at[s, half(h), block_of(j)]

    def send_stored(src, s, h, j, **where):
        copy = remote(src, hold(s, h, j), st_send.at[len(stored_sends)], st_recv.at[s, h, j], **where)
        copy.start()
        stored_sends.append(copy)

    def wait_stored(s, h, j):
        remote(hold(s, h, j), hold(s, h, j), st_send.at[0], st_recv.at[s, h, j], width=me).wait_recv()

    across = partner(my_store, bits[0]) if bits else None

    def held_before(stage):
        out = [my_store]
        for bit in bits[:stage]:
            out = out + [partner(s, bit) for s in out]
        return out

    def share_across():
        if bits:
            for j in range(chunks):
                for h in my_halves:
                    send_stored(st_hbm.at[half(h), block_of(j)], my_store, h, j, store=across)
            for j in range(chunks):
                send_stored(st_hbm.at[half(2), block_of(j)], my_store, 2, j, store=across)

    def share_rest():
        for bit in bits[1:]:
            for j in range(chunks):
                for h in range(3):
                    send_stored(st_hbm.at[half(h), block_of(j)], my_store, h, j, store=partner(my_store, bit))

    def pass_on(s, h, j, stage):
        for bit in bits[stage:]:
            send_stored(hold(s, h, j), s, h, j, store=partner(my_store, bit))

    def take_across(j):
        if bits and j < chunks:
            for h in my_halves:
                wait_stored(across, h, j)
                if groups == 2:
                    send_stored(hold(across, h, j), across, h, j, groups=1 - group)
                pass_on(across, h, j, 1)

    def take_group(j):
        if bits and groups == 2 and j < chunks:
            wait_stored(across, 1 - group, j)
            pass_on(across, 1 - group, j, 1)

    def take_middle(j):
        if bits and j < chunks:
            wait_stored(across, 2, j)
            pass_on(across, 2, j, 1)

    def take_rest(j):
        if j < chunks:
            for stage in range(1, len(bits)):
                for s in held_before(stage):
                    for h in range(3):
                        wait_stored(partner(s, bits[stage]), h, j)
                        pass_on(partner(s, bits[stage]), h, j, stage + 1)

    for copy in loads_w:
        copy.wait()

    own = None
    rs_copies = []
    for k in range(width):
        for copy in loads[k]:
            copy.wait()
        if k + 2 < width:
            for copy in loads[k + 2]:
                copy.start()
        if k == width - 1:
            load_inv.start()
            load_st.start()
            share_rest()
        part = (lax.dot_general(act[k], w_in[...], NT, preferred_element_type=F32)
                + lax.dot_general(grad[k], w_out[...], NT, preferred_element_type=F32))
        if k < width - 1:
            sbuf[k] = part.astype(BF16)
            copy = remote(sbuf.at[k], rbuf.at[k], rs_send.at[k], rs_recv.at[k],
                          width=wrap(me + 1 + k))
            if k == 0:
                pl.semaphore_wait(barrier, width + store - 2 + int(groups == 2))
            copy.start()
            if k == 0:
                share_across()
            rs_copies.append(copy)
        else:
            own = part
    @pl.when(me >= 0)
    def _():
        row_at = lax.broadcasted_iota(jnp.int32, (2 * rank, feat), 0)
        col_at = lax.broadcasted_iota(jnp.int32, (2 * rank, feat), 1)
        expand[...] = jnp.where(row_at - rank == col_at // rank, 1.0, 0.0).astype(BF16)
        belongs = ids_ref[...] == lax.broadcasted_iota(jnp.int32, (ex, ids_ref.shape[1]), 0)
        counts_ref[...] = jnp.broadcast_to(jnp.sum(belongs.astype(F32), axis=1, keepdims=True), counts_ref.shape)
        member[...] = belongs.astype(F32).astype(BF16)

    for k in range(width - 1):
        rs_copies[k].wait_recv()
        own = own + rbuf[k].astype(F32)
    fac[rows(me), :] = own.astype(BF16)
    ag_copies = []
    for k in sorted(range(width - 1), key=lambda k: abs(2 * (k + 1) - width)):
        copy = remote(fac.at[rows(me)], fac.at[rows(me)], ag_send.at[k], ag_recv.at[k],
                      width=wrap(me + 1 + k))
        copy.start()
        ag_copies.append(copy)
    take_across(0)
    counts = counts_ref[:, 0:1]
    for k in range(width - 1):
        sender = wrap(me + width - 1 - k)
        remote(fac.at[rows(me)], fac.at[rows(sender)], ag_send.at[k], ag_recv.at[k],
               width=sender).wait_recv()

    take_across(1)
    tile_row = lax.broadcasted_iota(jnp.int32, (2 * rank, 2 * rank), 0)
    tile_col = lax.broadcasted_iota(jnp.int32, (2 * rank, 2 * rank), 1)
    twice = jnp.where(tile_row == lax.rem(tile_col, rank), 1.0, 0.0).astype(BF16)
    block = 512
    act_twice = jnp.dot(fac[...], twice, preferred_element_type=F32)
    act_block = jnp.concatenate([act_twice] * (block // (2 * rank)), axis=1)

    @pl.loop(0, feat // block, unroll=True)
    def _(n):
        cols = pl.ds(pl.multiple_of(n * block, block), block)
        spread = jnp.dot(fac[...], expand[:, cols], preferred_element_type=F32)
        token_outer = (spread * act_block).astype(BF16)
        total = jnp.dot(member[...], token_outer, preferred_element_type=F32)
        pex[:, cols] = (total / counts).astype(BF16)

    take_across(2)
    take_group(0)
    load_inv.wait()

    rows_e = ex // pieces
    far_end = jnp.where(far > 0, width - 1, 0)
    near_end = width - 1 - far_end

    def unit(w, u, sliced):
        if sliced:
            return query.at[w, pl.ds(u * rows_e, rows_e), :]
        return query.at[w, :, pl.ds(u * piece, piece)]

    def along_width(w, u, step, sliced):
        return remote(unit(w, u, sliced), unit(w, u, sliced), z_send.at[(step + 1) // 2, w, u],
                      z_recv.at[w, u], width=me + step)

    def inside(w):
        return jnp.logical_and(w >= 0, w < width)

    def arrived(w, u, sliced):
        remote(unit(w, u, sliced), unit(w, u, sliced), z_send.at[0, w, u], z_recv.at[w, u],
               width=me).wait_recv()

    for p in range(pieces):
        value = lax.dot_general(pex[...], inv[p * piece:(p + 1) * piece, :], NT,
                                preferred_element_type=F32)
        query[me, :, p * piece:(p + 1) * piece] = value.astype(BF16)
        for step in (1, -1):
            @pl.when(inside(me + step))
            def _():
                along_width(me, p, step, False).start()

    def routes(d):
        return [(me + far * d, -far, far_end), (me - far * d, far, near_end)]

    def take(d):
        for w, step, end in routes(d):
            def pieces_on(w=w, step=step):
                for u in range(pieces):
                    arrived(w, u, False)

                    @pl.when(inside(me + step))
                    def _():
                        along_width(w, u, step, False).start()

            def slices_on(w=w, step=step):
                if d == 1:
                    for u in range(pieces):
                        arrived(w, u, False)
                for u in range(pieces):
                    if d > 1:
                        arrived(w, u, True)

                    @pl.when(inside(me + step))
                    def _():
                        along_width(w, u, step, True).start()

            if pieces == 1:
                pl.when(inside(w))(pieces_on)
            else:
                pl.when(jnp.logical_and(inside(w), w != end))(pieces_on)
                pl.when(w == end)(slices_on)

    def scores_of(w, first):
        for s in range(store):
            value = lax.dot_general(query[w], st[s, :, columns(w)], NT, preferred_element_type=F32)
            acc[s] = value if first else acc[s] + value

    def targets(e):
        here = pl.ds(e * rows_e, rows_e)
        there = pl.ds(pl.multiple_of(my_store * ex + e * rows_e, rows_e), rows_e)
        copies = []
        for k in range(1, store):
            to = lax.rem(my_store + k, store)
            copies.append(remote(acc.at[to, here], out_hbm.at[there], out_send.at[k, e],
                                 out_recv.at[k, e], store=to))
        return copies, pltpu.make_async_copy(acc.at[my_store, here], out_hbm.at[there], out_sem.at[e])

    take_across(3)
    take_middle(0)
    take_group(1)
    load_st.wait()
    take_rest(0)
    if width > 1:
        scores_of(me, True)
    take_middle(1)
    for d in range(1, width - 1):
        take(d)
        if d == 1:
            take_group(2)
            take_middle(2)
        take_rest(d)
        scores_of(order[d], d == 0)
        if d == 1:
            take_group(3)
            take_middle(3)

    if width > 1:
        take_rest(width - 1)
    last = order[width - 1]
    for e in range(pieces):
        if width > 1:
            @pl.when(near == 0)
            def _():
                if width > 2 and pieces > 1:
                    arrived(last, e, True)
                elif e == 0:
                    for u in range(pieces):
                        arrived(last, u, False)
        here = slice(e * rows_e, (e + 1) * rows_e)
        for s in range(store):
            value = lax.dot_general(query[last, here, :], st[s, :, columns(last)], NT,
                                    preferred_element_type=F32)
            acc[s, here, :] = acc[s, here, :] + value if width > 1 else value
        copies, mine = targets(e)
        for copy in copies:
            copy.start()
        mine.start()

    for e in range(pieces):
        copies, mine = targets(e)
        mine.wait()
        for k, copy in enumerate(copies, 1):
            source = lax.rem(my_store + store - k, store)
            lands = pl.ds(pl.multiple_of(source * ex + e * rows_e, rows_e), rows_e)
            remote(acc.at[source, pl.ds(e * rows_e, rows_e)], out_hbm.at[lands], out_send.at[k, e],
                   out_recv.at[k, e], store=source).wait_recv()
            copy.wait_send()
    for copy in rs_copies + ag_copies + stored_sends:
        copy.wait_send()
    for u in range(pieces):
        for step in (1, -1):
            @pl.when(inside(me + step))
            def _():
                along_width(me, u, step, False).wait_send()
    for d in range(1, width - 1):
        for w, step, end in routes(d):
            for sliced in ((False, True) if pieces > 1 else (False,)):
                ok = jnp.logical_and(inside(w), inside(me + step))
                if pieces > 1:
                    ok = jnp.logical_and(ok, (w == end) if sliced else (w != end))

                @pl.when(ok)
                def _():
                    for u in range(pieces):
                        along_width(w, u, step, sliced).wait_send()


def partner(s, bit):
    return s + bit - 2 * bit * lax.rem(s // bit, 2)


def body(activations, out_grads, example_of, proj_in, proj_out, inverse_curvature, stored):
    width = lax.axis_size("width")
    store = lax.axis_size("store")
    groups = lax.axis_size("groups")
    tokens, depth = activations.shape
    rank = proj_in.shape[1]
    part, feat = inverse_curvature.shape
    chunk = tokens // width
    piece = min(part, 256)
    pieces = part // piece
    n_rows = stored.shape[0]
    chunks = width if width <= 4 else 1
    assert store & (store - 1) == 0
    hbm = pl.BlockSpec(memory_space=pl.ANY)
    vmem = pl.BlockSpec(memory_space=pltpu.VMEM)
    dma = pltpu.SemaphoreType.DMA
    return pl.pallas_call(
        functools.partial(kernel, (width, store, groups, chunk, pieces, piece)),
        out_shape=jax.ShapeDtypeStruct((store * EX_DEV, n_rows), F32),
        in_specs=[hbm, hbm, vmem, hbm, hbm, hbm, hbm],
        out_specs=hbm,
        scratch_shapes=[
            pltpu.VMEM((width, chunk, depth), BF16),
            pltpu.VMEM((width, chunk, depth), BF16),
            pltpu.VMEM((2 * rank, depth), BF16),
            pltpu.VMEM((2 * rank, depth), BF16),
            pltpu.VMEM((part, feat), BF16),
            pltpu.VMEM((store, n_rows, feat), BF16),
            pltpu.VMEM((width - 1, chunk, 2 * rank), BF16),
            pltpu.VMEM((width - 1, chunk, 2 * rank), BF16),
            pltpu.VMEM((tokens, 2 * rank), BF16),
            pltpu.VMEM((2 * rank, feat), BF16),
            pltpu.VMEM((EX_DEV, tokens), BF16),
            pltpu.VMEM((EX_DEV, 128), F32),
            pltpu.VMEM((EX_DEV, feat), BF16),
            pltpu.VMEM((width, EX_DEV, part), BF16),
            pltpu.VMEM((store, EX_DEV, n_rows), F32),
            dma((4 + 2 * width,)),
            dma((width - 1,)),
            dma((width - 1,)),
            dma((width - 1,)),
            dma((width - 1,)),
            dma((2, width, pieces)),
            dma((width, pieces)),
            dma((4 * chunks * store * store.bit_length(),)),
            dma((store, 3, chunks)),
            dma((store, pieces)),
            dma((store, pieces)),
            dma((pieces,)),
        ],
        compiler_params=pltpu.CompilerParams(
            collective_id=0, has_side_effects=True, vmem_limit_bytes=60 * 1024 * 1024),
        name="logra",
    )(activations, out_grads, example_of, proj_in.T, proj_out.T, inverse_curvature, stored)


def solution(mesh):
    return jax.shard_map(
        body,
        mesh=mesh,
        in_specs=(
            P(("groups", "store"), "width"),
            P(("groups", "store"), "width"),
            P(("groups", "store"), None),
            P("width", None),
            P("width", None),
            P("width", None),
            P(("width", "store"), None),
        ),
        out_specs=P("groups", ("width", "store")),
        check_vma=False,
    )
```

time: 55.1 us -> 53.9 us (0.978)
  Pallas kernels: 52.5 us -> 51.8 us
    pallas_call x1, Pallas kernels: 52.5 us -> 51.8 us  [body(): pl.pallas_call(functools.partial(kernel, (width, store, groups, chunk, pi...]
where the time goes in v2:
time: 53.9 us; the launch traced here: 53.7 us
  Pallas kernels  51.8 us (96%)
  local copies, waits for them, and re-layouts  1.87 us (3%)
    pallas_call x1, Pallas kernels, body(): pl.pallas_call(functools.partial(kernel, (width, store, groups, chunk, pi...  51.8 us
    unnamed x1, local copies, waits for them, and re-layouts  1.87 us

profile of v2, /device:TPU:0, one launch (start us, length us, event | category | flops | bytes accessed | tf_op | source)
XLA Modules:
  0.0 53.7 jit_solution(6021252544966229205)
XLA Ops:
  0.0 51.8 %logra.1 = f32[512,256]{1,0:T(8,128)} custom-call(bf16[1024,2048]{1,0:T(8,128)(2,1)} %act_hbm.1, bf16[1024,2048]{1,0:T(8,128)(2,1)} %grad_hbm.1, s32[1,1024]{1,0:T(1,128)} %ids_ref.1, bf16[64,2048]{1,0:T(8,128)(2,1)} %bitcast.2, bf16[64,2048]{1,0:T(8,128)(2,1)} %bitcast.3, bf16[1024,4096]{1,0:T(8,128)(2,1)} %inv_hbm.1, bf16[256,4096]{1,0:T(8,128)(2,1)} %st_hbm.1), custom_call_target="tpu_custom_call" | custom-call | tf_op jit(solution)/shard_map/logra/pallas_call | solution.py:407
  51.8 1.9 %copy.9 = f32[512,256]{1,0:T(8,128)} copy(f32[512,256]{1,0:T(8,128)} %logra.1) | data formatting | bytes 1048576

commit v3 on v2

--- a/solution.py
+++ b/solution.py
@@ -225,13 +225,13 @@
     twice = jnp.where(tile_row == lax.rem(tile_col, rank), 1.0, 0.0).astype(BF16)
     block = 512
     act_twice = jnp.dot(fac[...], twice, preferred_element_type=F32)
-    act_block = jnp.concatenate([act_twice] * (block // (2 * rank)), axis=1)
+    act_block = jnp.concatenate([act_twice.astype(BF16)] * (block // (2 * rank)), axis=1)
 
     @pl.loop(0, feat // block, unroll=True)
     def _(n):
         cols = pl.ds(pl.multiple_of(n * block, block), block)
         spread = jnp.dot(fac[...], expand[:, cols], preferred_element_type=F32)
-        token_outer = (spread * act_block).astype(BF16)
+        token_outer = spread.astype(BF16) * act_block
         total = jnp.dot(member[...], token_outer, preferred_element_type=F32)
         pex[:, cols] = (total / counts).astype(BF16)
 
@@ -317,14 +317,13 @@
     take_across(3)
     take_middle(0)
     take_group(1)
-    load_st.wait()
-    take_rest(0)
-    if width > 1:
-        scores_of(me, True)
     take_middle(1)
     for d in range(1, width - 1):
         take(d)
         if d == 1:
+            load_st.wait()
+            take_rest(0)
+            scores_of(me, True)
             take_group(2)
             take_middle(2)
         take_rest(d)

time: 53.9 us -> 53.3 us (0.989)
  Pallas kernels: 51.8 us -> 51.2 us
    pallas_call x1, Pallas kernels: 51.8 us -> 51.2 us  [body(): pl.pallas_call(functools.partial(kernel, (width, store, groups, chunk, pi...]
where the time goes in v3:
time: 53.3 us; the launch traced here: 53.1 us
  Pallas kernels  51.2 us (96%)
  local copies, waits for them, and re-layouts  1.87 us (4%)
    pallas_call x1, Pallas kernels, body(): pl.pallas_call(functools.partial(kernel, (width, store, groups, chunk, pi...  51.2 us
    unnamed x1, local copies, waits for them, and re-layouts  1.87 us

profile of v3, /device:TPU:0, one launch (start us, length us, event | category | flops | bytes accessed | tf_op | source)
XLA Modules:
  0.0 53.1 jit_solution(15222990728058717101)
XLA Ops:
  0.0 51.2 %logra.1 = f32[512,256]{1,0:T(8,128)} custom-call(bf16[1024,2048]{1,0:T(8,128)(2,1)} %act_hbm.1, bf16[1024,2048]{1,0:T(8,128)(2,1)} %grad_hbm.1, s32[1,1024]{1,0:T(1,128)} %ids_ref.1, bf16[64,2048]{1,0:T(8,128)(2,1)} %bitcast.2, bf16[64,2048]{1,0:T(8,128)(2,1)} %bitcast.3, bf16[1024,4096]{1,0:T(8,128)(2,1)} %inv_hbm.1, bf16[256,4096]{1,0:T(8,128)(2,1)} %st_hbm.1), custom_call_target="tpu_custom_call" | custom-call | tf_op jit(solution)/shard_map/logra/pallas_call | solution.py:406
  51.2 1.9 %copy.9 = f32[512,256]{1,0:T(8,128)} copy(f32[512,256]{1,0:T(8,128)} %logra.1) | data formatting | bytes 1048576

commit v4 on v3

--- a/solution.py
+++ b/solution.py
@@ -268,6 +268,9 @@
             def _():
                 along_width(me, p, step, False).start()
 
+    for copy in rs_copies + ag_copies:
+        copy.wait_send()
+
     def routes(d):
         return [(me + far * d, -far, far_end), (me - far * d, far, near_end)]
 
@@ -354,16 +357,7 @@
             copy.start()
         mine.start()
 
-    for e in range(pieces):
-        copies, mine = targets(e)
-        mine.wait()
-        for k, copy in enumerate(copies, 1):
-            source = lax.rem(my_store + store - k, store)
-            lands = pl.ds(pl.multiple_of(source * ex + e * rows_e, rows_e), rows_e)
-            remote(acc.at[source, pl.ds(e * rows_e, rows_e)], out_hbm.at[lands], out_send.at[k, e],
-                   out_recv.at[k, e], store=source).wait_recv()
-            copy.wait_send()
-    for copy in rs_copies + ag_copies + stored_sends:
+    for copy in stored_sends:
         copy.wait_send()
     for u in range(pieces):
         for step in (1, -1):
@@ -381,6 +375,15 @@
                 def _():
                     for u in range(pieces):
                         along_width(w, u, step, sliced).wait_send()
+    for e in range(pieces):
+        copies, mine = targets(e)
+        mine.wait()
+        for k, copy in enumerate(copies, 1):
+            source = lax.rem(my_store + store - k, store)
+            lands = pl.ds(pl.multiple_of(source * ex + e * rows_e, rows_e), rows_e)
+            remote(acc.at[source, pl.ds(e * rows_e, rows_e)], out_hbm.at[lands], out_send.at[k, e],
+                   out_recv.at[k, e], store=source).wait_recv()
+            copy.wait_send()
 
 
 def partner(s, bit):

time: 53.3 us -> 53.1 us (level)
  no operation moved by 1% of the time
where the time goes in v4:
time: 53.1 us; the launch traced here: 53 us
  Pallas kernels  51.1 us (96%)
  local copies, waits for them, and re-layouts  1.87 us (4%)
    pallas_call x1, Pallas kernels, body(): pl.pallas_call(functools.partial(kernel, (width, store, groups, chunk, pi...  51.1 us
    unnamed x1, local copies, waits for them, and re-layouts  1.87 us

profile of v4, /device:TPU:0, one launch (start us, length us, event | category | flops | bytes accessed | tf_op | source)
XLA Modules:
  0.0 53.0 jit_solution(12639874071961088039)
XLA Ops:
  0.0 51.1 %logra.1 = f32[512,256]{1,0:T(8,128)} custom-call(bf16[1024,2048]{1,0:T(8,128)(2,1)} %act_hbm.1, bf16[1024,2048]{1,0:T(8,128)(2,1)} %grad_hbm.1, s32[1,1024]{1,0:T(1,128)} %ids_ref.1, bf16[64,2048]{1,0:T(8,128)(2,1)} %bitcast.2, bf16[64,2048]{1,0:T(8,128)(2,1)} %bitcast.3, bf16[1024,4096]{1,0:T(8,128)(2,1)} %inv_hbm.1, bf16[256,4096]{1,0:T(8,128)(2,1)} %st_hbm.1), custom_call_target="tpu_custom_call" | custom-call | tf_op jit(solution)/shard_map/logra/pallas_call | solution.py:409
  51.1 1.9 %copy.9 = f32[512,256]{1,0:T(8,128)} copy(f32[512,256]{1,0:T(8,128)} %logra.1) | data formatting | bytes 1048576
